TPU v7x, 32 devices: a whole 2x2x4 slice. The times are simulated.
32 devices in a mesh: rows: 16 (over z, y, x), cols: 2 (over core).
Axes of the slice: x: 2, y: 2, z: 4, core: 2. Of those that a mesh axis runs over, the one named last changes fastest.
Arguments:
- quantized: bfloat16 [3072, 384, 128], P('rows', 'cols'), may hold values from 0 to 127, as said below
- scales: bfloat16 [3072, 384], P('rows', 'cols'), may hold values from 0 to 1, as said below
- mode_one: float32 [3072, 32], P('rows'), may hold values from 0 to 40
- mode_two: bfloat16 [384, 32], P('cols'), may hold values from 0 to 1, as said below
- mode_three: bfloat16 [4096, 32], replicated, may hold values from 0 to 0.29882812
- core_tensor: float32 [32, 32, 32], P('rows'), may hold values from 0.0002 to 0.004
- slab_index: int32 [1], replicated, may hold values from 0 to 31
Outputs:
- new_one: float32 [3072, 32], P('rows')
- new_core: float32 [32, 32, 32], P('rows')
Inputs may be any that keep to these rules, and one draw needn't show every extreme that they name: `quantized`: nonnegative integer values of an int8 quantization. `scales`: positive. `mode_two`: nonnegative.
All inputs are finite; a program needn't handle non-finite values.
Results may differ from a plain program's by a relative error of at most 0.0017.
Values sent between devices are 32-bit elements; how exact they have to be, the bound alone decides.
A program may use at most 64 MiB of HBM per device.

v0:
```python
import jax
import jax.numpy as jnp
from jax import lax
from jax.sharding import PartitionSpec as P

SLAB = 128


def weight_gram(core_whole, gram_two, gram_three):
    highest = lax.Precision.HIGHEST
    left = jnp.einsum("rab,ac->rcb", core_whole, gram_two, precision=highest)
    left = jnp.einsum("rcb,bd->rcd", left, gram_three, precision=highest)
    flat = core_whole.reshape(core_whole.shape[0], -1)
    return jnp.dot(left.reshape(flat.shape), flat.T, precision=highest)


def hals_sweep(current, target, coupling):
    highest = lax.Precision.HIGHEST

    def column(position, values):
        where = jnp.asarray(position).astype(jnp.int32)
        weights = lax.dynamic_slice_in_dim(coupling, where, 1, 1)[:, 0]
        diagonal = lax.dynamic_index_in_dim(weights, where, 0, keepdims=False)
        wanted = lax.dynamic_slice_in_dim(target, where, 1, 1)[:, 0]
        before = lax.dynamic_slice_in_dim(values, where, 1, 1)[:, 0]
        fitted = jnp.dot(values, weights, precision=highest)
        after = jnp.maximum(before + (wanted - fitted) / diagonal, 0.0)
        return lax.dynamic_update_slice_in_dim(values, after[:, None], where, 1)

    return lax.fori_loop(0, coupling.shape[0], column, current)


def local(quantized, scales, mode_one, mode_two, mode_three, core_tensor, slab_index):
    highest = lax.Precision.HIGHEST
    whole_core = lax.all_gather(core_tensor, "rows", axis=0, tiled=True)
    flat_core = whole_core.reshape(whole_core.shape[0], -1)
    offset = slab_index[0] * SLAB
    chosen = lax.dynamic_slice_in_dim(mode_three, offset, SLAB, 0)
    tensor = quantized * scales[:, :, None]
    folded = jnp.einsum("jr,ijk->irk", mode_two, tensor, preferred_element_type=jnp.float32).astype(
        jnp.bfloat16
    )
    partial_value = jnp.einsum("irk,ks->irs", folded, chosen, preferred_element_type=jnp.float32)
    partial_value = partial_value.reshape(partial_value.shape[0], -1)
    gram_local = jnp.dot(mode_two.T, mode_two, preferred_element_type=jnp.float32)
    gram_three = jnp.dot(chosen.T, chosen, preferred_element_type=jnp.float32)
    local_target = jnp.dot(partial_value, flat_core.T, precision=highest)
    target, gram_two = lax.psum((local_target, gram_local), "cols")
    coupling = weight_gram(whole_core, gram_two, gram_three)
    updated = hals_sweep(mode_one, target, coupling)
    squares = jnp.sum(updated * updated, axis=0)
    counted = mode_one.shape[0] * lax.axis_size("rows")
    totals = lax.psum(squares, "rows")
    spread = jnp.sqrt(totals / counted + 1e-06)
    normed = updated / spread
    local_rank = core_tensor.shape[0]
    owned = lax.dynamic_slice_in_dim(spread, lax.axis_index("rows") * local_rank, local_rank, 0)
    return (normed, core_tensor * owned[:, None, None])


def solution(mesh):
    in_specs = (
        P("rows", "cols", None),
        P("rows", "cols"),
        P("rows", None),
        P("cols", None),
        P(),
        P("rows", None, None),
        P(),
    )
    out_specs = (P("rows", None), P("rows", None, None))
    return jax.shard_map(local, mesh=mesh, in_specs=in_specs, out_specs=out_specs, check_vma=False)
```

profile of v0, /device:TPU:0, one launch (start us, length us, event | category | flops | bytes accessed | tf_op | source)
XLA Modules:
  0.0 148.8 jit_solution(15536030878287488232)
XLA Ops:
  1.4 8.6 %fusion.10 = bf16[192,32,128]{2,1,0:T(8,128)(2,1)S(1)} fusion(bf16[192,192,128]{2,1,0:T(8,128)(2,1)} %param.9, bf16[192,192]{1,0:T(8,128)(2,1)} %param.10, bf16[192,32]{0,1:T(8,128)(2,1)} %param.12), kind=kOutput, calls=%fused_computation.12 | convolution fusion | flops 321650688 | bytes 11096064 | tf_op jit(solution)/shard_map/jr,ijk->irk/dot_general | solution.py:40
  10.0 1.1 fusion.8
  11.1 45.3 %all_gather.3 = f32[32,32,32]{2,1,0:T(8,128)S(1)} all-gather(f32[2,32,32]{2,1,0:T(8,128)S(1)} %copy-done.2), channel_id=1, replica_groups=mesh['rows'=16,'cols'=2] {'rows'}, dimensions={0}, use_global_device_ids=true | all-gather | bytes 139264 | tf_op jit(solution)/shard_map/all_gather | solution.py:35
  56.5 1.1 convolution_bitcast_fusion.1
  57.7 3.5 %all-reduce = (f32[192,32]{0,1:T(8,128)S(1)}, f32[32,32]{1,0:T(8,128)S(1)}) all-reduce(f32[192,32]{0,1:T(8,128)S(1)} %convolution_bitcast_fusion.1, f32[32,32]{1,0:T(8,128)S(1)} %fusion.24), channel_id=1, replica_groups=mesh['rows'=16,'cols'=2] {'cols'}, use_global_device_ids=true, to_apply=%region_1.0 | all-reduce | flops 7168 | bytes 57344 | tf_op jit(solution)/shard_map/psum | solution.py:48
  62.0 0.9 fusion.13
  62.9 0.8 convolution_bitcast_fusion.2
  63.7 46.9 %while.16 = (s32[]{:T(128)}, f32[192,32]{0,1:T(8,128)S(1)}, f32[192,32]{0,1:T(8,128)S(1)}, f32[32,32]{0,1:T(8,128)S(1)}, s32[]{:T(128)}, /*index=5*/s32[]{:T(128)}, s32[]{:T(128)}) while((s32[]{:T(128)}, f32[192,32]{0,1:T(8,128)S(1)}, f32[192,32]{0,1:T(8,128)S(1)}, f32[32,32]{0,1:T(8,128)S(1)}, s32[]{:T(128)}, /*index=5*/s32[]{:T(128)}, ...), condition=%wide.region_3.4_spmd, body=%wide.region_2.3_spmd.sunk | while | flops 74499 | bytes 41849 | solution.py:30
  64.5 0.7 fusion.37
  65.9 0.7 fusion.37
  67.4 0.7 fusion.37
  68.9 0.7 fusion.37
  76.2 0.7 fusion.37
  77.7 0.7 fusion.37
  79.1 0.7 fusion.37
  89.4 0.7 fusion.37
  90.9 0.7 fusion.37
  92.4 0.7 fusion.37
  104.1 0.7 fusion.37
  105.6 0.7 fusion.37
  107.0 0.7 fusion.37
  110.8 36.6 %psum.23 = f32[32]{0:T(128)S(1)} all-reduce(f32[32]{0:T(128)S(1)} %multiply_reduce_fusion), channel_id=1, replica_groups=mesh['rows'=16,'cols'=2] {'rows'}, use_global_device_ids=true, to_apply=%region_5.6 | all-reduce | flops 32 | bytes 256 | tf_op jit(solution)/shard_map/psum | solution.py:53
  147.4 0.7 broadcast_divide_fusion
  148.1 0.7 broadcast_multiply_fusion
  (161 shorter events, 38.4 us)
Async XLA Ops:
  0.6 9.4 %copy-start = (bf16[4096,32]{0,1:T(8,128)(2,1)S(1)}, bf16[4096,32]{0,1:T(8,128)(2,1)}, u32[]{:S(2)}) copy-start(bf16[4096,32]{0,1:T(8,128)(2,1)} %param.13) | copy-start | bytes 786436
  0.6 56.9 %copy-start.3 = (bf16[192,32]{0,1:T(8,128)(2,1)S(1)}, bf16[192,32]{0,1:T(8,128)(2,1)}, u32[]{:S(2)}) copy-start(bf16[192,32]{0,1:T(8,128)(2,1)} %param.12) | copy-start | bytes 36868
  0.7 10.5 %copy-start.2 = (f32[2,32,32]{2,1,0:T(8,128)S(1)}, f32[2,32,32]{2,1,0:T(8,128)}, u32[]{:S(2)}) copy-start(f32[2,32,32]{2,1,0:T(8,128)} %param.14) | copy-start | bytes 24580
  1.4 62.4 %copy-start.1 = (f32[192,32]{0,1:T(8,128)S(1)}, f32[192,32]{0,1:T(8,128)}, u32[]{:S(2)}) copy-start(f32[192,32]{0,1:T(8,128)} %param.11) | copy-start | bytes 73732
where the time goes:
time: 149 us
  blocking collectives  85.5 us (57%)
  other arithmetic  22.3 us (15%)
  local copies, waits for them, and re-layouts  20.7 us (14%)
  matrix products  17.8 us (12%)
    all_gather x1, blocking collectives, local(): whole_core = lax.all_gather(core_tensor, 'rows', axis=0, tiled=True)  45.3 us
    psum x1, blocking collectives, local(): totals = lax.psum(squares, 'rows')  36.6 us
    max x32, other arithmetic, column(): after = jnp.maximum(before + (wanted - fitted) / diagonal, 0.0)  20.8 us
    dynamic_slice x32, local copies, waits for them, and re-layouts, column(): diagonal = lax.dynamic_index_in_dim(weights, where, 0, keepdims=False)  18.9 us
    dot_general x1, matrix products, local(): jnp.einsum('jr,ijk->irk', mode_two, tensor, preferred_element_type=jnp.fl...  8.62 us
    dot_general x32, matrix products, column(): fitted = jnp.dot(values, weights, precision=highest)  4.4 us
    psum x1, blocking collectives, local(): target, gram_two = lax.psum((local_target, gram_local), 'cols')  3.54 us

commit v1 on v0

--- a/solution.py
+++ b/solution.py
@@ -4,6 +4,28 @@
 from jax.sharding import PartitionSpec as P
 
 SLAB = 128
+
+
+def in_order(parts, dim):
+    parts = jnp.moveaxis(parts, 0, dim)
+    shape = parts.shape
+    return parts.reshape(*shape[:dim], shape[dim] * shape[dim + 1], *shape[dim + 2 :])
+
+
+def grow_blocks(x, axis):
+    size = lax.axis_size(axis)
+    blocks = x[None]
+    for level in range(size.bit_length() - 1):
+        apart = 1 << level
+        other = lax.ppermute(blocks, axis, [(i, i ^ apart) for i in range(size)])
+        both = jnp.stack([blocks, other])
+        upper = lax.axis_index(axis) >> level & 1
+        blocks = jnp.where(upper == 0, both, both[::-1]).reshape(-1, *x.shape)
+    return blocks
+
+
+def collect(x, axis, dim):
+    return in_order(grow_blocks(x, axis), dim)
 
 
 def weight_gram(core_whole, gram_two, gram_three):
@@ -32,7 +54,7 @@
 
 def local(quantized, scales, mode_one, mode_two, mode_three, core_tensor, slab_index):
     highest = lax.Precision.HIGHEST
-    whole_core = lax.all_gather(core_tensor, "rows", axis=0, tiled=True)
+    whole_core = collect(core_tensor, "rows", 0)
     flat_core = whole_core.reshape(whole_core.shape[0], -1)
     offset = slab_index[0] * SLAB
     chosen = lax.dynamic_slice_in_dim(mode_three, offset, SLAB, 0)

time: 149 us -> 131 us (0.88)
  blocking collectives: 85.5 us -> 44.5 us
  waiting for transfers between devices: 0 us -> 13.4 us
  starting transfers between devices: 0 us -> 9.52 us
  matrix products: 17.8 us -> 16.3 us
    all_gather x1 -> x0, blocking collectives: 45.3 us -> none  [local(): whole_core = lax.all_gather(core_tensor, 'rows', axis=0, tiled=True)]
    ppermute x0 -> x4, waiting for transfers between devices: none -> 13.4 us  [grow_blocks(): other = lax.ppermute(blocks, axis, [(i, i ^ apart) for i in range(size)])]
    ppermute x0 -> x4, starting transfers between devices: none -> 9.52 us  [grow_blocks(): other = lax.ppermute(blocks, axis, [(i, i ^ apart) for i in range(size)])]
    psum x1, blocking collectives: 36.6 us -> 40.9 us  [local(): totals = lax.psum(squares, 'rows')]
  transfers between devices with their start and end apart: 0 -> 4, of which waited for: 0 -> 3; matrix products, arithmetic and copies ran while one was open for 0% -> 7% of each run, Pallas kernels for 0% -> 0%
where the time goes in v1:
time: 131 us
  blocking collectives  44.5 us (34%)
  other arithmetic  23.3 us (18%)
  local copies, waits for them, and re-layouts  21.2 us (16%)
  matrix products  16.3 us (12%)
  waiting for transfers between devices  13.4 us (10%)
  starting transfers between devices  9.52 us (7%)
  between operations  1.47 us (1%)
    psum x1, blocking collectives, local(): totals = lax.psum(squares, 'rows')  40.9 us
    max x32, other arithmetic, column(): after = jnp.maximum(before + (wanted - fitted) / diagonal, 0.0)  20.8 us
    dynamic_slice x32, local copies, waits for them, and re-layouts, column(): diagonal = lax.dynamic_index_in_dim(weights, where, 0, keepdims=False)  18.9 us
    ppermute x4, waiting for transfers between devices, grow_blocks(): other = lax.ppermute(blocks, axis, [(i, i ^ apart) for i in range(size)])  13.4 us
    ppermute x4, starting transfers between devices, grow_blocks(): other = lax.ppermute(blocks, axis, [(i, i ^ apart) for i in range(size)])  9.52 us
    dot_general x1, matrix products, local(): jnp.einsum('jr,ijk->irk', mode_two, tensor, preferred_element_type=jnp.fl...  8.46 us
    dot_general x32, matrix products, column(): fitted = jnp.dot(values, weights, precision=highest)  4.4 us
    psum x1, blocking collectives, local(): target, gram_two = lax.psum((local_target, gram_local), 'cols')  3.54 us
  transfers between devices with their start and end apart: 4, of which 3 were waited for; matrix products, arithmetic and copies ran while one was open for 7% of the time, Pallas kernels for 0%

profile of v1, /device:TPU:0, one launch (start us, length us, event | category | flops | bytes accessed | tf_op | source)
XLA Modules:
  0.0 130.7 jit_solution(16704111454479774722)
XLA Ops:
  0.7 3.0 %collective-permute-start = (f32[1,2,32,32]{3,2,1,0:T(8,128)}, f32[1,2,32,32]{3,2,1,0:T(8,128)S(1)}, u32[]{:S(2)}, u32[]{:S(2)}) collective-permute-start(f32[1,2,32,32]{3,2,1,0:T(8,128)} %bitcast.69), channel_id=1, source_target_pairs={{0,2},{2,0},{4,6},{6,4},{8,10},{10,8},{12,14},{14,12},{16,18},{18,... | collective-permute-start | bytes 24584 | tf_op jit(solution)/shard_map/ppermute | solution.py:20
  3.7 2.1 %collective-permute-done = f32[1,2,32,32]{3,2,1,0:T(8,128)S(1)} collective-permute-done((f32[1,2,32,32]{3,2,1,0:T(8,128)}, f32[1,2,32,32]{3,2,1,0:T(8,128)S(1)}, u32[]{:S(2)}, u32[]{:S(2)}) %collective-permute-start) | collective-permute-done | bytes 8224 | tf_op jit(solution)/shard_map/ppermute | solution.py:20
  5.8 0.8 pad_maximum_fusion.3
  6.6 2.1 %collective-permute-start.1 = (f32[2,2,32,32]{3,2,1,0:T(8,128)S(1)}, f32[2,2,32,32]{3,2,1,0:T(8,128)S(1)}, u32[]{:S(2)}, u32[]{:S(2)}) collective-permute-start(f32[2,2,32,32]{3,2,1,0:T(8,128)S(1)} %get-tuple-element.148), channel_id=1, source_target_pairs={{0,4},{2,6},{4,0},{6,2},{8,12},{10,14},{12,8},{14,10},{16,20},{18,... | collective-permute-start | bytes 49160 | tf_op jit(solution)/shard_map/ppermute | solution.py:20
  8.7 8.5 %fusion.10 = bf16[192,32,128]{2,1,0:T(8,128)(2,1)S(1)} fusion(bf16[192,192,128]{2,1,0:T(8,128)(2,1)} %param.9, bf16[192,192]{1,0:T(8,128)(2,1)} %param.10, bf16[192,32]{0,1:T(8,128)(2,1)} %param.12), kind=kOutput, calls=%fused_computation.12 | convolution fusion | flops 321650688 | bytes 11096064 | tf_op jit(solution)/shard_map/jr,ijk->irk/dot_general | solution.py:62
  17.9 1.6 %collective-permute-start.2 = (f32[4,2,32,32]{3,2,1,0:T(8,128)S(1)}, f32[4,2,32,32]{3,2,1,0:T(8,128)S(1)}, u32[]{:S(2)}, u32[]{:S(2)}) collective-permute-start(f32[4,2,32,32]{3,2,1,0:T(8,128)S(1)} %bitcast.66), channel_id=1, source_target_pairs={{0,8},{2,10},{4,12},{6,14},{8,0},{10,2},{12,4},{14,6},{16,24},{18,... | collective-permute-start | bytes 98312 | tf_op jit(solution)/shard_map/ppermute | solution.py:20
  19.5 1.1 fusion.8
  20.6 2.3 %collective-permute-done.2 = f32[4,2,32,32]{3,2,1,0:T(8,128)S(1)} collective-permute-done((f32[4,2,32,32]{3,2,1,0:T(8,128)S(1)}, f32[4,2,32,32]{3,2,1,0:T(8,128)S(1)}, u32[]{:S(2)}, u32[]{:S(2)}) %collective-permute-start.2) | collective-permute-done | bytes 32800 | tf_op jit(solution)/shard_map/ppermute | solution.py:20
  23.0 2.8 %collective-permute-start.3 = (f32[8,2,32,32]{3,2,1,0:T(8,128)S(1)}, f32[8,2,32,32]{3,2,1,0:T(8,128)S(1)}, u32[]{:S(2)}, u32[]{:S(2)}) collective-permute-start(f32[8,2,32,32]{3,2,1,0:T(8,128)S(1)} %bitcast.64), channel_id=1, source_target_pairs={{0,16},{2,18},{4,20},{6,22},{8,24},{10,26},{12,28},{14,30},{16,0},... | collective-permute-start | bytes 196616 | tf_op jit(solution)/shard_map/ppermute | solution.py:20
  26.0 9.0 %collective-permute-done.3 = f32[8,2,32,32]{3,2,1,0:T(8,128)S(1)} collective-permute-done((f32[8,2,32,32]{3,2,1,0:T(8,128)S(1)}, f32[8,2,32,32]{3,2,1,0:T(8,128)S(1)}, u32[]{:S(2)}, u32[]{:S(2)}) %collective-permute-start.3) | collective-permute-done | bytes 65568 | tf_op jit(solution)/shard_map/ppermute | solution.py:20
  36.0 3.5 %all-reduce = (f32[192,32]{0,1:T(8,128)S(1)}, f32[32,32]{1,0:T(8,128)S(1)}) all-reduce(f32[192,32]{0,1:T(8,128)S(1)} %fusion.22, f32[32,32]{1,0:T(8,128)S(1)} %fusion.23), channel_id=1, replica_groups=mesh['rows'=16,'cols'=2] {'cols'}, use_global_device_ids=true, to_apply=%region_1.2 | all-reduce | flops 7168 | bytes 57344 | tf_op jit(solution)/shard_map/psum | solution.py:70
  41.3 46.9 %while.16 = (s32[]{:T(128)}, f32[192,32]{0,1:T(8,128)S(1)}, f32[192,32]{0,1:T(8,128)S(1)}, f32[32,32]{0,1:T(8,128)S(1)}, s32[]{:T(128)}, /*index=5*/s32[]{:T(128)}, s32[]{:T(128)}) while((s32[]{:T(128)}, f32[192,32]{0,1:T(8,128)S(1)}, f32[192,32]{0,1:T(8,128)S(1)}, f32[32,32]{0,1:T(8,128)S(1)}, s32[]{:T(128)}, /*index=5*/s32[]{:T(128)}, ...), condition=%wide.region_3.4_spmd, body=%wide.region_2.3_spmd.sunk | while | flops 74499 | bytes 41857 | solution.py:52
  46.4 0.7 fusion.41
  47.9 0.7 fusion.41
  49.4 0.7 fusion.41
  59.6 0.7 fusion.41
  61.1 0.7 fusion.41
  62.6 0.7 fusion.41
  74.3 0.7 fusion.41
  75.8 0.7 fusion.41
  77.2 0.7 fusion.41
  88.3 40.9 %psum.23 = f32[32]{0:T(128)S(1)} all-reduce(f32[32]{0:T(128)S(1)} %multiply_reduce_fusion), channel_id=1, replica_groups=mesh['rows'=16,'cols'=2] {'rows'}, use_global_device_ids=true, to_apply=%region_5.6 | all-reduce | flops 32 | bytes 256 | tf_op jit(solution)/shard_map/psum | solution.py:75
  129.2 0.7 broadcast_divide_fusion
  130.0 0.7 broadcast_multiply_fusion
  (178 shorter events, 43.1 us)
Async XLA Ops:
  0.6 18.9 %copy-start = (bf16[4096,32]{0,1:T(8,128)(2,1)S(1)}, bf16[4096,32]{0,1:T(8,128)(2,1)}, u32[]{:S(2)}) copy-start(bf16[4096,32]{0,1:T(8,128)(2,1)} %param.13) | copy-start | bytes 786436
  0.6 25.1 %copy-start.3 = (bf16[192,32]{0,1:T(8,128)(2,1)S(1)}, bf16[192,32]{0,1:T(8,128)(2,1)}, u32[]{:S(2)}) copy-start(bf16[192,32]{0,1:T(8,128)(2,1)} %param.12) | copy-start | bytes 36868
  0.7 5.1 %collective-permute-start = (f32[1,2,32,32]{3,2,1,0:T(8,128)}, f32[1,2,32,32]{3,2,1,0:T(8,128)S(1)}, u32[]{:S(2)}, u32[]{:S(2)}) collective-permute-start(f32[1,2,32,32]{3,2,1,0:T(8,128)} %bitcast.69), channel_id=1, source_target_pairs={{0,2},{2,0},{4,6},{6,4},{8,10},{10,8},{12,14},{14,12},{16,18},{18,... | collective-permute-start | bytes 24584 | tf_op jit(solution)/shard_map/ppermute | solution.py:20
  6.6 34.7 %copy-start.1 = (f32[192,32]{0,1:T(8,128)S(1)}, f32[192,32]{0,1:T(8,128)}, u32[]{:S(2)}) copy-start(f32[192,32]{0,1:T(8,128)} %param.11) | copy-start | bytes 73732
  6.6 11.3 %collective-permute-start.1 = (f32[2,2,32,32]{3,2,1,0:T(8,128)S(1)}, f32[2,2,32,32]{3,2,1,0:T(8,128)S(1)}, u32[]{:S(2)}, u32[]{:S(2)}) collective-permute-start(f32[2,2,32,32]{3,2,1,0:T(8,128)S(1)} %get-tuple-element.148), channel_id=1, source_target_pairs={{0,4},{2,6},{4,0},{6,2},{8,12},{10,14},{12,8},{14,10},{16,20},{18,... | collective-permute-start | bytes 49160 | tf_op jit(solution)/shard_map/ppermute | solution.py:20
  17.1 112.9 %copy-start.2 = (f32[2,32,32]{2,1,0:T(8,128)S(1)}, f32[2,32,32]{2,1,0:T(8,128)}, u32[]{:S(2)}) copy-start(f32[2,32,32]{2,1,0:T(8,128)} %param.14) | copy-start | bytes 24580
  17.9 5.0 %collective-permute-start.2 = (f32[4,2,32,32]{3,2,1,0:T(8,128)S(1)}, f32[4,2,32,32]{3,2,1,0:T(8,128)S(1)}, u32[]{:S(2)}, u32[]{:S(2)}) collective-permute-start(f32[4,2,32,32]{3,2,1,0:T(8,128)S(1)} %bitcast.66), channel_id=1, source_target_pairs={{0,8},{2,10},{4,12},{6,14},{8,0},{10,2},{12,4},{14,6},{16,24},{18,... | collective-permute-start | bytes 98312 | tf_op jit(solution)/shard_map/ppermute | solution.py:20
  23.0 12.0 %collective-permute-start.3 = (f32[8,2,32,32]{3,2,1,0:T(8,128)S(1)}, f32[8,2,32,32]{3,2,1,0:T(8,128)S(1)}, u32[]{:S(2)}, u32[]{:S(2)}) collective-permute-start(f32[8,2,32,32]{3,2,1,0:T(8,128)S(1)} %bitcast.64), channel_id=1, source_target_pairs={{0,16},{2,18},{4,20},{6,22},{8,24},{10,26},{12,28},{14,30},{16,0},... | collective-permute-start | bytes 196616 | tf_op jit(solution)/shard_map/ppermute | solution.py:20
